TPU v7x, 32 devices: a whole 2x2x4 slice. The times are simulated.
32 devices in a mesh: group: 4 (over x, core), mp: 8 (over z, y).
Axes of the slice: x: 2, y: 2, z: 4, core: 2. Of those that a mesh axis runs over, the one named last changes fastest.
Arguments:
- tokens: bfloat16 [4096, 8192], P(('group', 'mp')), may hold values from -36 to 36
- cached_update: bfloat16 [4096, 8192], P('group', 'mp'), may hold values from -3 to 3
- norm_gain: float32 [8192], replicated, may hold values from 0.25 to 1.75
- gate_weight: bfloat16 [8192, 14336], P('group', 'mp'), may hold values from -0.0625 to 0.0625
- up_weight: bfloat16 [8192, 14336], P('group', 'mp'), may hold values from -0.0625 to 0.0625
- down_weight: bfloat16 [14336, 8192], P('mp', 'group'), may hold values from -0.0625 to 0.0625
- stale_blocks: int32 [4, 2], P('group'), may hold values from -1 to 7, as said below
- stale_count: int32 [4], replicated, may hold values from 0 to 2, as said below
- lengths: int32 [4], P('group'), may hold values from 512 to 1024, as said below
Outputs:
- refreshed: bfloat16 [4096, 8192], P('group', 'mp')
Inputs may be any that keep to these rules, and one draw needn't show every extreme that they name: `stale_count`: the counts sum to exactly 4. At least a quarter of the groups have 2, at least a quarter have none. A group's count never exceeds the number of its blocks that begin below its length. `stale_blocks`: row g holds stale_count[g] distinct block numbers, each of a block that begins below lengths[g], in any order, then -1 in the other places. Some group lists block 7. `lengths`: some request has 1024 tokens.
All inputs are finite; a program needn't handle non-finite values.
Results may differ from a plain program's by a relative error of at most 0.0035.
Values may be sent and summed in bfloat16 or wider, within the bound.
A program may use at most 256 MiB of HBM per device.

v0:
```python
import jax
import jax.numpy as jnp
from jax import lax
from jax.sharding import PartitionSpec as P

BLK = 128
epsilon = 1e-05


def normalize(row_data, norm_gain):
    values = row_data.astype(jnp.float32)
    mean_sq = jnp.mean(values * values, axis=-1, keepdims=True)
    return (values * lax.rsqrt(mean_sq + epsilon) * norm_gain).astype(jnp.bfloat16)


def refresh(slots, norm_gain, gate_weight, up_weight, down_weight):
    slot_count = slots.shape[0]
    full_rows = lax.all_gather(slots, "mp", axis=2, tiled=True)
    row_data = full_rows.reshape(slot_count * BLK, full_rows.shape[2])
    normed = normalize(row_data, norm_gain)
    gate_vals = jnp.dot(
        normed,
        lax.all_gather(gate_weight, "group", axis=0, tiled=True),
        preferred_element_type=jnp.float32,
    )
    up_vals = jnp.dot(
        normed,
        lax.all_gather(up_weight, "group", axis=0, tiled=True),
        preferred_element_type=jnp.float32,
    )
    hidden = (jax.nn.silu(gate_vals) * up_vals).astype(jnp.bfloat16)
    partial_value = jnp.dot(
        hidden,
        lax.all_gather(down_weight, "group", axis=1, tiled=True),
        preferred_element_type=jnp.float32,
    )
    update = lax.psum_scatter(
        partial_value.astype(jnp.bfloat16), "mp", scatter_dimension=1, tiled=True
    ).astype(jnp.float32)
    return update.reshape(slot_count, BLK, update.shape[1])


def body(
    tokens,
    cached_update,
    norm_gain,
    gate_weight,
    up_weight,
    down_weight,
    stale_blocks,
    stale_count,
    lengths,
):
    n_group = lax.axis_size("group")
    columns = lax.all_to_all(tokens, "mp", split_axis=1, concat_axis=0, tiled=True)
    seq_rows, col_width = columns.shape
    block_total = seq_rows // BLK
    column_blocks = columns.reshape(block_total, BLK, col_width)
    group_id = lax.axis_index("group")
    group_ids = jnp.arange(n_group, dtype=jnp.int32)
    own_mask = group_ids == group_id
    own_count = jnp.sum(jnp.where(own_mask, stale_count, 0))
    own_list = stale_blocks[0]
    list_size = stale_blocks.shape[1]
    block_ids = jnp.arange(block_total, dtype=jnp.int32)
    picker = (own_list[:, None] == block_ids[None, :]).astype(jnp.bfloat16)
    own_rows = jnp.einsum(
        "pb,brc->prc", picker, column_blocks, preferred_element_type=jnp.float32
    ).astype(jnp.bfloat16)
    results = refresh(own_rows, norm_gain, gate_weight, up_weight, down_weight)
    positions = jnp.arange(list_size, dtype=jnp.int32)
    listed = (own_list[None, :] == block_ids[:, None]) & (positions[None, :] < own_count)
    block_update = jnp.einsum(
        "bp,prc->brc", listed.astype(jnp.float32), results, precision=lax.Precision.HIGHEST
    )
    stale_rows = jnp.any(listed, axis=1)[:, None, None]
    row_pos = block_ids[:, None] * BLK + jnp.arange(BLK, dtype=jnp.int32)[None, :]
    live_rows = (row_pos < lengths[0])[:, :, None]
    cache_blocks = cached_update.reshape(block_total, BLK, col_width).astype(jnp.float32)
    combined = column_blocks.astype(jnp.float32) + jnp.where(stale_rows, block_update, cache_blocks)
    refreshed = jnp.where(live_rows, combined, jnp.float32(0.0))
    return refreshed.astype(jnp.bfloat16).reshape(seq_rows, col_width)


def solution(mesh):
    in_specs = (
        P(("group", "mp"), None),
        P("group", "mp"),
        P(),
        P("group", "mp"),
        P("group", "mp"),
        P("mp", "group"),
        P("group", None),
        P(),
        P("group"),
    )
    out_specs = P("group", "mp")
    return jax.shard_map(body, mesh=mesh, in_specs=in_specs, out_specs=out_specs, check_vma=False)
```

profile of v0, /device:TPU:0, one launch (start us, length us, event | category | flops | bytes accessed | tf_op | source)
XLA Modules:
  0.0 816.9 jit_solution(3097391666787981656)
XLA Ops:
  6.5 0.0 all-gather.5.cloned.1.call-start
  6.5 4.1 copy.28
  10.6 0.0 copy-start.4
  10.6 2.9 copy.29
  13.5 55.3 %all_to_all.16 = bf16[128,8,1024]{2,0,1:T(8,128)(2,1)S(1)} all-to-all(bf16[128,8,1024]{2,0,1:T(8,128)(2,1)S(1)} %copy.29), channel_id=1, replica_groups=mesh['group'=4,'mp'=8] {'mp'}, dimensions={1} | all-to-all | bytes 4194304 | tf_op jit(solution)/shard_map/all_to_all | solution.py:55
  68.8 0.0 copy-start.1
  68.8 1.3 copy-done.1
  70.1 0.0 copy-done.4
  70.1 1.4 fusion.6
  71.6 0.9 copy.53
  72.5 0.0 all-gather.5.cloned.1.call-update
  72.6 0.0 all-gather.7.cloned.1.call-start
  72.6 0.7 all-gather.7.cloned.1.call-update
  73.3 0.0 all-gather.11.cloned.1.call-start
  73.3 0.7 all-gather.11.cloned.1.call-update
  74.0 0.0 copy-start.3
  74.0 0.0 all-gather.9.cloned.1.call-start
  74.1 0.5 all-gather.9.cloned.1.call-update
  74.6 0.2 reduce-scatter.2.cloned.1.call-start
  74.9 69.6 %all-gather.5.cloned.1.call-done = bf16[2,128,8192]{2,1,0:T(8,128)(2,1)} async-done(((bf16[2,128,1024]{2,1,0:T(8,128)(2,1)}), bf16[2,128,8192]{2,1,0:T(8,128)(2,1)}) %all-gather.5.cloned.1.call-update) | async-done | bytes 4194320 | tf_op jit(solution)/shard_map/all_gather | solution.py:18
  144.5 0.0 copy-start
  144.5 3.3 multiply_reduce_fusion
  147.8 0.0 copy-done.3
  147.8 0.2 copy-done
  147.9 3.4 fusion.1
  151.3 171.3 %all-gather.7.cloned.1.call-done = bf16[8192,1792]{1,0:T(8,128)(2,1)} async-done(((bf16[2048,1792]{1,0:T(8,128)(2,1)}), bf16[8192,1792]{1,0:T(8,128)(2,1)}) %all-gather.7.cloned.1.call-update) | async-done | bytes 29360144 | tf_op jit(solution)/shard_map/all_gather | solution.py:23
  322.6 17.9 %fusion.26 = f32[256,1792]{1,0:T(8,128)S(1)} fusion(bf16[256,8192]{1,0:T(8,128)(2,1)} %fusion.1, bf16[8192,1792]{1,0:T(8,128)(2,1)} %all-gather.7.cloned.1.call-done), kind=kOutput, calls=%fused_computation.38 | convolution fusion | flops 7516192768 | bytes 35389440 | tf_op jit(solution)/shard_map/dot_general | solution.py:21
  340.5 161.7 %all-gather.11.cloned.1.call-done = bf16[1792,8192]{1,0:T(8,128)(2,1)} async-done(((bf16[1792,2048]{1,0:T(8,128)(2,1)}), bf16[1792,8192]{1,0:T(8,128)(2,1)}) %all-gather.11.cloned.1.call-update) | async-done | bytes 29360144 | tf_op jit(solution)/shard_map/all_gather | solution.py:34
  502.2 179.4 %all-gather.9.cloned.1.call-done = bf16[8192,1792]{1,0:T(8,128)(2,1)} async-done(((bf16[2048,1792]{1,0:T(8,128)(2,1)}), bf16[8192,1792]{1,0:T(8,128)(2,1)}) %all-gather.9.cloned.1.call-update) | async-done | bytes 29360144 | tf_op jit(solution)/shard_map/all_gather | solution.py:28
  681.6 29.4 %convolution_convert_fusion = bf16[256,8192]{1,0:T(8,128)(2,1)} fusion(bf16[1792,8192]{1,0:T(8,128)(2,1)} %all-gather.11.cloned.1.call-done, bf16[256,8192]{1,0:T(8,128)(2,1)} %fusion.1, bf16[8192,1792]{1,0:T(8,128)(2,1)} %all-gather.9.cloned.1.call-done, f32[256,1792]{1,0:T(8,128)S(1)} %fusion.26), kind=kOutput, calls=%fused_computation | convolution fusion | flops 15037235200 | bytes 68943872 | tf_op jit(solution)/shard_map/dot_general | solution.py:32
  711.0 0.0 reduce-scatter.2.cloned.1.call-update
  711.0 0.0 copy-start.6
  711.0 0.0 copy-start.5
  711.1 0.0 copy-start.2
  711.1 4.2 convert.2
  715.9 0.0 copy-done.6
  715.9 0.6 fusion.22
  716.5 0.5 iota_compare_fusion
  717.1 0.0 copy-done.5
  717.1 0.1 fusion.20
  717.2 82.7 %reduce-scatter.2.cloned.1.call-done = bf16[256,1024]{1,0:T(8,128)(2,1)} async-done(((bf16[256,8192]{1,0:T(8,128)(2,1)}), bf16[256,1024]{1,0:T(8,128)(2,1)}) %reduce-scatter.2.cloned.1.call-update) | async-done | bytes 524304 | tf_op jit(solution)/shard_map/reduce_scatter | solution.py:37
  799.9 0.0 copy-done.2
  799.9 8.0 fusion.4
  807.9 2.5 copy.36
  (3 shorter events, 0.0 us)
Async XLA Ops:
  6.5 138.0 %all-gather.5.cloned.1.call-start = ((), (), s32[]{:S(2)}) async-start(), calls=%async_computation.2 | async-start | bytes 4718592 | tf_op jit(solution)/shard_map/all_gather | solution.py:18
  10.6 59.5 %copy-start.4 = (s32[1,2]{1,0:T(1,128)S(1)}, s32[1,2]{1,0:T(1,128)}, u32[]{:S(2)}) copy-start(s32[1,2]{1,0:T(1,128)} %param.15) | copy-start | bytes 28
  68.8 1.3 copy-start.1
  72.6 250.1 %all-gather.7.cloned.1.call-start = ((), (), s32[]{:S(2)}) async-start(), calls=%async_computation.3 | async-start | bytes 36700160 | tf_op jit(solution)/shard_map/all_gather | solution.py:23
  73.3 428.9 %all-gather.11.cloned.1.call-start = ((), (), s32[]{:S(2)}) async-start(), calls=%async_computation.5 | async-start | bytes 36700160 | tf_op jit(solution)/shard_map/all_gather | solution.py:34
  74.0 73.7 %copy-start.3 = (f32[8192]{0:T(1024)S(1)}, f32[8192]{0:T(1024)}, u32[]{:S(2)}) copy-start(f32[8192]{0:T(1024)} %param.11) | copy-start | bytes 98308
  74.0 607.6 %all-gather.9.cloned.1.call-start = ((), (), s32[]{:S(2)}) async-start(), calls=%async_computation.4 | async-start | bytes 36700160 | tf_op jit(solution)/shard_map/all_gather | solution.py:28
  74.6 725.3 %reduce-scatter.2.cloned.1.call-start = ((), (), s32[]{:S(2)}) async-start(), calls=%async_computation.6 | async-start | bytes 4718592 | tf_op jit(solution)/shard_map/reduce_scatter | solution.py:37
  144.5 3.4 copy-start
  711.0 4.9 copy-start.6
  711.0 6.0 copy-start.5
  711.1 88.8 %copy-start.2 = (bf16[128,8,1024]{2,0,1:T(8,128)(2,1)S(1)}, bf16[128,8,1024]{2,0,1:T(8,128)(2,1)}, u32[]{:S(2)}) copy-start(bf16[128,8,1024]{2,0,1:T(8,128)(2,1)} %copy-done.1) | copy-start | bytes 6291460
Sparse Core Ops, SparseCore 0:
  72.7 71.7 all-gather.4
  146.1 176.5 all-gather.6
  324.2 177.9 all-gather.10
  503.6 177.9 all-gather.8
  711.2 88.6 reduce-scatter.1
where the time goes:
time: 817 us
  waiting for transfers between devices  667 us (82%)
  matrix products  56.7 us (7%)
  blocking collectives  55.3 us (7%)
  between operations  13.9 us (2%)
  other arithmetic  12.1 us (1%)
  local copies, waits for them, and re-layouts  11.9 us (1%)
    all_gather x1, waiting for transfers between devices, refresh(): lax.all_gather(up_weight, 'group', axis=0, tiled=True)  179 us
    all_gather x1, waiting for transfers between devices, refresh(): lax.all_gather(gate_weight, 'group', axis=0, tiled=True)  171 us
    all_gather x1, waiting for transfers between devices, refresh(): lax.all_gather(down_weight, 'group', axis=1, tiled=True)  162 us
    reduce_scatter x1, waiting for transfers between devices, refresh(): lax.psum_scatter(partial_value.astype(jnp.bfloat16), 'mp', scatter_dimens...  82.7 us
    all_gather x1, waiting for transfers between devices, refresh(): full_rows = lax.all_gather(slots, 'mp', axis=2, tiled=True)  69.6 us
    all_to_all x1, blocking collectives, body(): lax.all_to_all(tokens, 'mp', split_axis=1, concat_axis=0, tiled=True)  55.3 us
    dot_general x1, matrix products, refresh(): jnp.dot(hidden, lax.all_gather(down_weight, 'group', axis=1, tiled=True),...  29.4 us
    dot_general x1, matrix products, refresh(): jnp.dot(normed, lax.all_gather(gate_weight, 'group', axis=0, tiled=True),...  17.9 us
  transfers between devices with their start and end apart: 5, of which 5 were waited for; matrix products, arithmetic and copies ran while one was open for 4% of the time, Pallas kernels for 0%

commit v1 on v0

--- a/solution.py
+++ b/solution.py
@@ -52,7 +52,20 @@
     lengths,
 ):
     n_group = lax.axis_size("group")
-    columns = lax.all_to_all(tokens, "mp", split_axis=1, concat_axis=0, tiled=True)
+
+    def drive_cubes_all(chunk, net_axis, array_axis, axis_no):
+        near = jnp.concatenate(
+            lax.all_to_all(
+                jnp.stack(jnp.split(chunk, lax.axis_size(net_axis), axis=array_axis)),
+                axis_name=net_axis,
+                split_axis=0,
+                concat_axis=0,
+            ),
+            axis=axis_no,
+        )
+        return near
+
+    columns = drive_cubes_all(tokens, "mp", array_axis=1, axis_no=0)
     seq_rows, col_width = columns.shape
     block_total = seq_rows // BLK
     column_blocks = columns.reshape(block_total, BLK, col_width)

time: 817 us -> 814 us (level)
  no operation moved by 1% of the time
where the time goes in v1:
time: 814 us
  waiting for transfers between devices  666 us (82%)
  matrix products  56.8 us (7%)
  blocking collectives  55.3 us (7%)
  between operations  14 us (2%)
  other arithmetic  12.3 us (2%)
  local copies, waits for them, and re-layouts  9.05 us (1%)
    all_gather x1, waiting for transfers between devices, refresh(): lax.all_gather(up_weight, 'group', axis=0, tiled=True)  179 us
    all_gather x1, waiting for transfers between devices, refresh(): lax.all_gather(gate_weight, 'group', axis=0, tiled=True)  171 us
    all_gather x1, waiting for transfers between devices, refresh(): lax.all_gather(down_weight, 'group', axis=1, tiled=True)  162 us
    reduce_scatter x1, waiting for transfers between devices, refresh(): lax.psum_scatter(partial_value.astype(jnp.bfloat16), 'mp', scatter_dimens...  82.4 us
    all_gather x1, waiting for transfers between devices, refresh(): full_rows = lax.all_gather(slots, 'mp', axis=2, tiled=True)  69.6 us
    all_to_all x1, blocking collectives, drive_cubes_all(): lax.all_to_all(jnp.stack(jnp.split(chunk, lax.axis_size(net_axis), axis=a...  55.3 us
    dot_general x1, matrix products, refresh(): jnp.dot(hidden, lax.all_gather(down_weight, 'group', axis=1, tiled=True),...  29.4 us
    dot_general x1, matrix products, refresh(): jnp.dot(normed, lax.all_gather(gate_weight, 'group', axis=0, tiled=True),...  18 us
  transfers between devices with their start and end apart: 5, of which 5 were waited for; matrix products, arithmetic and copies ran while one was open for 4% of the time, Pallas kernels for 0%

profile of v1, /device:TPU:0, one launch (start us, length us, event | category | flops | bytes accessed | tf_op | source)
XLA Modules:
  0.0 814.1 jit_solution(5898609872480830965)
XLA Ops:
  6.5 0.0 copy-start.3
  6.5 0.0 all-gather.5.cloned.1.call-start
  6.5 1.1 bitcast_dynamic-update-slice_fusion.7
  7.7 1.0 bitcast_dynamic-update-slice_fusion.6
  8.6 1.0 bitcast_dynamic-update-slice_fusion.5
  9.6 1.0 bitcast_dynamic-update-slice_fusion.4
  10.6 0.0 copy-done.3
  10.7 0.0 copy-start.5
  10.7 55.3 %all_to_all.5 = bf16[8,128,1024]{2,1,0:T(8,128)(2,1)S(1)} all-to-all(bf16[8,128,1024]{2,1,0:T(8,128)(2,1)S(1)} %bitcast_dynamic-update-slice_fusion), channel_id=1, replica_groups=mesh['group'=4,'mp'=8] {'mp'}, dimensions={0} | all-to-all | bytes 4194304 | tf_op jit(solution)/shard_map/all_to_all | solution.py:58
  66.1 0.0 copy-start.1
  66.1 1.3 copy-done.1
  67.4 0.0 copy-done.5
  67.4 1.4 fusion.6
  68.8 0.9 copy.58
  69.8 0.0 all-gather.5.cloned.1.call-update
  69.8 0.0 all-gather.7.cloned.1.call-start
  69.8 0.7 all-gather.7.cloned.1.call-update
  70.5 0.0 all-gather.11.cloned.1.call-start
  70.6 0.7 all-gather.11.cloned.1.call-update
  71.3 0.0 all-gather.9.cloned.1.call-start
  71.3 0.0 copy-start.4
  71.3 0.5 all-gather.9.cloned.1.call-update
  71.9 0.2 reduce-scatter.2.cloned.1.call-start
  72.1 69.6 %all-gather.5.cloned.1.call-done = bf16[2,128,8192]{2,1,0:T(8,128)(2,1)} async-done(((bf16[2,128,1024]{2,1,0:T(8,128)(2,1)}), bf16[2,128,8192]{2,1,0:T(8,128)(2,1)}) %all-gather.5.cloned.1.call-update) | async-done | bytes 4194320 | tf_op jit(solution)/shard_map/all_gather | solution.py:18
  141.7 0.0 copy-start
  141.7 3.3 multiply_reduce_fusion
  145.0 0.0 copy-done.4
  145.0 0.2 copy-done
  145.2 3.4 fusion.1
  148.6 171.3 %all-gather.7.cloned.1.call-done = bf16[8192,1792]{1,0:T(8,128)(2,1)} async-done(((bf16[2048,1792]{1,0:T(8,128)(2,1)}), bf16[8192,1792]{1,0:T(8,128)(2,1)}) %all-gather.7.cloned.1.call-update) | async-done | bytes 29360144 | tf_op jit(solution)/shard_map/all_gather | solution.py:23
  319.9 18.0 %fusion.25 = f32[256,1792]{1,0:T(8,128)S(1)} fusion(bf16[256,8192]{1,0:T(8,128)(2,1)} %fusion.1, bf16[8192,1792]{1,0:T(8,128)(2,1)} %all-gather.7.cloned.1.call-done), kind=kOutput, calls=%fused_computation.45 | convolution fusion | flops 7516192768 | bytes 35389440 | tf_op jit(solution)/shard_map/dot_general | solution.py:21
  337.8 161.6 %all-gather.11.cloned.1.call-done = bf16[1792,8192]{1,0:T(8,128)(2,1)} async-done(((bf16[1792,2048]{1,0:T(8,128)(2,1)}), bf16[1792,8192]{1,0:T(8,128)(2,1)}) %all-gather.11.cloned.1.call-update) | async-done | bytes 29360144 | tf_op jit(solution)/shard_map/all_gather | solution.py:34
  499.4 179.4 %all-gather.9.cloned.1.call-done = bf16[8192,1792]{1,0:T(8,128)(2,1)} async-done(((bf16[2048,1792]{1,0:T(8,128)(2,1)}), bf16[8192,1792]{1,0:T(8,128)(2,1)}) %all-gather.9.cloned.1.call-update) | async-done | bytes 29360144 | tf_op jit(solution)/shard_map/all_gather | solution.py:28
  678.9 29.4 %convolution_convert_fusion = bf16[256,8192]{1,0:T(8,128)(2,1)} fusion(bf16[1792,8192]{1,0:T(8,128)(2,1)} %all-gather.11.cloned.1.call-done, bf16[256,8192]{1,0:T(8,128)(2,1)} %fusion.1, bf16[8192,1792]{1,0:T(8,128)(2,1)} %all-gather.9.cloned.1.call-done, f32[256,1792]{1,0:T(8,128)S(1)} %fusion.25), kind=kOutput, calls=%fused_computation | convolution fusion | flops 15037235200 | bytes 68943872 | tf_op jit(solution)/shard_map/dot_general | solution.py:32
  708.3 0.0 reduce-scatter.2.cloned.1.call-update
  708.3 0.0 copy-start.7
  708.3 0.0 copy-start.6
  708.3 0.0 copy-start.2
  708.3 4.2 convert.2
  713.2 0.0 copy-done.7
  713.2 0.7 fusion.21
  713.9 0.7 iota_compare_fusion
  714.6 0.0 copy-done.6
  714.6 0.1 fusion.19
  714.7 82.4 %reduce-scatter.2.cloned.1.call-done = bf16[256,1024]{1,0:T(8,128)(2,1)} async-done(((bf16[256,8192]{1,0:T(8,128)(2,1)}), bf16[256,1024]{1,0:T(8,128)(2,1)}) %reduce-scatter.2.cloned.1.call-update) | async-done | bytes 524304 | tf_op jit(solution)/shard_map/reduce_scatter | solution.py:37
  797.2 0.0 copy-done.2
  797.2 8.0 fusion.4
  805.1 2.5 copy.43
  (7 shorter events, 0.1 us)
Async XLA Ops:
  6.5 4.0 copy-start.3
  6.5 135.2 %all-gather.5.cloned.1.call-start = ((), (), s32[]{:S(2)}) async-start(), calls=%async_computation.2 | async-start | bytes 4718592 | tf_op jit(solution)/shard_map/all_gather | solution.py:18
  10.7 56.7 %copy-start.5 = (s32[1,2]{1,0:T(1,128)S(1)}, s32[1,2]{1,0:T(1,128)}, u32[]{:S(2)}) copy-start(s32[1,2]{1,0:T(1,128)} %param.15) | copy-start | bytes 28
  66.1 1.3 copy-start.1
  69.8 250.1 %all-gather.7.cloned.1.call-start = ((), (), s32[]{:S(2)}) async-start(), calls=%async_computation.3 | async-start | bytes 36700160 | tf_op jit(solution)/shard_map/all_gather | solution.py:23
  70.5 428.9 %all-gather.11.cloned.1.call-start = ((), (), s32[]{:S(2)}) async-start(), calls=%async_computation.5 | async-start | bytes 36700160 | tf_op jit(solution)/shard_map/all_gather | solution.py:34
  71.3 607.6 %all-gather.9.cloned.1.call-start = ((), (), s32[]{:S(2)}) async-start(), calls=%async_computation.4 | async-start | bytes 36700160 | tf_op jit(solution)/shard_map/all_gather | solution.py:28
  71.3 73.7 %copy-start.4 = (f32[8192]{0:T(1024)S(1)}, f32[8192]{0:T(1024)}, u32[]{:S(2)}) copy-start(f32[8192]{0:T(1024)} %param.11) | copy-start | bytes 98308
  71.9 725.3 %reduce-scatter.2.cloned.1.call-start = ((), (), s32[]{:S(2)}) async-start(), calls=%async_computation.6 | async-start | bytes 4718592 | tf_op jit(solution)/shard_map/reduce_scatter | solution.py:37
  141.7 3.4 copy-start
  708.3 4.9 copy-start.7
  708.3 6.3 copy-start.6
  708.3 88.8 %copy-start.2 = (bf16[8,128,1024]{2,1,0:T(8,128)(2,1)S(1)}, bf16[8,128,1024]{2,1,0:T(8,128)(2,1)}, u32[]{:S(2)}) copy-start(bf16[8,128,1024]{2,1,0:T(8,128)(2,1)} %copy-done.1) | copy-start | bytes 6291460
Sparse Core Ops, SparseCore 0:
  69.9 71.7 all-gather.4
  143.3 176.5 all-gather.6
  321.4 177.9 all-gather.10
  500.9 177.9 all-gather.8
  708.4 88.6 reduce-scatter.1
